TPU v7x, 128 devices: a whole 4x4x4 slice. The times are simulated.
128 devices in a mesh: sky: 16 (over z, y), exp: 8 (over x, core).
Axes of the slice: x: 4, y: 4, z: 4, core: 2. Of those that a mesh axis runs over, the one named last changes fastest.
Arguments:
- sky_model: bfloat16 [4096, 1024], P('sky'), may hold values from -6 to 6
- exposure_data: bfloat16 [2048, 128, 128], P(('sky', 'exp')), may hold values from -6 to 6
- pixel_mask: int32 [2048, 128, 128], P(('sky', 'exp')), may hold values 0 or 1
- block_owner: int32 [2048, 1], P(('sky', 'exp')), may hold values from 0 to 15; in each aligned block of 16 rows (0 to 15, 16 to 31, ...) at most 2 rows name the same one
- block_local: int32 [2048], P(('sky', 'exp')), may hold values from 0 to 15
- psf_cell: int32 [2048], P(('sky', 'exp')), may hold values from 0 to 15
- psf_table: bfloat16 [128, 1681], P('exp'), may hold values from -0.15625 to 0.15625
Outputs:
- model_grad: float32 [4096, 1024], P('sky', 'exp')
- residual: bfloat16 [2048, 128, 128], P(('sky', 'exp'))
Inputs may be any that keep to these rules, and one draw needn't show every extreme that they name: `block_owner`: among the pieces of one device no sky index is named more than 2 times.
All inputs are finite; a program needn't handle non-finite values. No bound on the sum of `pixel_mask` on one device may be relied on, other than what follows from the above.
Results may differ from a plain program's by a relative error of at most 0.014.
Values may be sent and summed in bfloat16 or wider, within the bound.
No kernel may reach another device: no remote copies, remote signals or barrier semaphores. Data moves between devices by JAX's collectives and lax.ppermute only.
A program may use at most 64 MiB of HBM per device.

v0:
```python
import jax
import jax.numpy as jnp
from jax import lax
from jax.sharding import PartitionSpec as P

B = 128
PSF = 41
HALO = 20
CAP = 2


def from_behind(x, axis, by):
    devices = lax.axis_size(axis)
    pairs = [(i, i + by) for i in range(devices) if 0 <= i + by < devices]
    return lax.ppermute(x, axis, pairs)


def banded_table(out_cols):
    width = out_cols + PSF - 1
    tap_index = lax.broadcasted_iota(jnp.int32, (PSF, width, out_cols), 0)
    column = lax.broadcasted_iota(jnp.int32, (PSF, width, out_cols), 1)
    target = lax.broadcasted_iota(jnp.int32, (PSF, width, out_cols), 2)
    return (column - target == tap_index).astype(jnp.bfloat16)


def correlate(field, kernel, table, out_rows):
    out_cols = table.shape[2]
    width = field.shape[1]
    banded = jnp.einsum("ab,bcj->caj", kernel, table, preferred_element_type=jnp.float32).astype(
        jnp.bfloat16
    )
    spread = jnp.dot(
        field, banded.reshape(width, PSF * out_cols), preferred_element_type=jnp.float32
    )
    total = spread[0:out_rows, 0:out_cols]
    for offset in range(1, PSF):
        total = (
            total + spread[offset : offset + out_rows, offset * out_cols : (offset + 1) * out_cols]
        )
    return total


def fold_blocks(per_block, block_rows, per_row):
    extent = B + 2 * HALO
    margin = 2 * HALO
    grid = per_block.reshape(block_rows, per_row, extent, extent)
    col_main = grid[..., :B].transpose(0, 2, 1, 3).reshape(block_rows, extent, per_row * B)
    col_tail = jnp.pad(grid[..., B:], ((0, 0), (0, 0), (0, 0), (0, B - margin)))
    col_tail = col_tail.transpose(0, 2, 1, 3).reshape(block_rows, extent, per_row * B)
    width = per_row * B + margin
    columns = (
        jnp.pad(col_main, ((0, 0), (0, 0), (0, margin)))
        + jnp.pad(col_tail, ((0, 0), (0, 0), (B, 0)))[:, :, :width]
    )
    row_main = columns[:, :B].reshape(block_rows * B, width)
    row_tail = jnp.pad(columns[:, B:], ((0, 0), (0, B - margin), (0, 0))).reshape(
        block_rows * B, width
    )
    height = block_rows * B + margin
    return jnp.pad(row_main, ((0, margin), (0, 0))) + jnp.pad(row_tail, ((B, 0), (0, 0)))[:height]


def shards(sky_model, exposure_data, pixel_mask, block_owner, block_local, psf_cell, psf_table):
    sky_count = lax.axis_size("sky")
    extent = B + 2 * HALO
    stripe_rows = sky_model.shape[0]
    stripe_cols = sky_model.shape[1]
    per_row = stripe_cols // B
    block_rows = stripe_rows // B
    block_total = block_rows * per_row
    piece_count = exposure_data.shape[0]
    slot_total = sky_count * CAP
    owner_sky = block_owner[:, 0]
    earlier = lax.broadcasted_iota(jnp.int32, (piece_count, piece_count), 1) < lax.broadcasted_iota(
        jnp.int32, (piece_count, piece_count), 0
    )
    same_owner = owner_sky[:, None] == owner_sky[None, :]
    rank_within = jnp.sum((same_owner & earlier).astype(jnp.int32), axis=1)
    slot_index = owner_sky * CAP + rank_within
    requests = (
        jnp.full((slot_total,), -1, jnp.int32)
        .at[slot_index]
        .set(block_local)
        .reshape(sky_count, CAP)
    )
    cell_count = psf_table.shape[0]
    cell_onehot = (psf_cell[:, None] == lax.broadcasted_iota(jnp.int32, (1, cell_count), 1)).astype(
        jnp.bfloat16
    )
    kernels_flat = jnp.dot(cell_onehot, psf_table, preferred_element_type=jnp.float32).astype(
        jnp.bfloat16
    )
    forward_table = banded_table(B)
    adjoint_table = banded_table(extent)

    def per_piece(item):
        patch, kernel, observed, keep = item
        predicted = correlate(patch, kernel, forward_table, B)
        residual = (keep.astype(jnp.float32) * (predicted - observed.astype(jnp.float32))).astype(
            jnp.bfloat16
        )
        widened = jnp.pad(residual, 2 * HALO)
        adjoint = correlate(widened, kernel[::-1, ::-1], adjoint_table, extent)
        return (residual, adjoint)

    whole = lax.all_gather(sky_model, "sky", axis=0, tiled=True)
    padded = jnp.pad(whole, HALO)
    row_start = (owner_sky * block_rows + block_local // per_row) * B
    col_start = block_local % per_row * B

    def cut_patch(row_first, col_first):
        return lax.dynamic_slice(padded, (row_first, col_first), (extent, extent))

    patches = jax.vmap(cut_patch)(row_start, col_start)
    kernels = kernels_flat.reshape(piece_count, PSF, PSF)
    residuals, adjoints = lax.map(per_piece, (patches, kernels, exposure_data, pixel_mask))
    outgoing = jnp.zeros((slot_total, extent, extent), jnp.float32).at[slot_index].set(adjoints)
    outgoing = outgoing.reshape(sky_count, CAP, extent, extent)
    received, received_ids = (
        lax.all_to_all(
            outgoing.astype(jnp.bfloat16), "sky", split_axis=0, concat_axis=0, tiled=True
        ).astype(outgoing.dtype),
        lax.all_to_all(requests, "sky", split_axis=0, concat_axis=0, tiled=True),
    )
    contributions = received.reshape(slot_total, extent, extent)
    asked_ids = received_ids.reshape(slot_total)
    selector = (asked_ids[:, None] == lax.broadcasted_iota(jnp.int32, (1, block_total), 1)).astype(
        jnp.float32
    )
    per_block = jnp.einsum("nl,nuv->luv", selector, contributions, precision=lax.Precision.HIGHEST)
    canvas = fold_blocks(per_block, block_rows, per_row)
    core = canvas[:, HALO : HALO + stripe_cols]
    from_below = from_behind(core[:HALO].astype(jnp.bfloat16), "sky", -1).astype(jnp.float32)
    from_above = from_behind(core[stripe_rows + HALO :].astype(jnp.bfloat16), "sky", 1).astype(
        jnp.float32
    )
    middle = core[HALO : stripe_rows + HALO]
    folded = (
        middle
        + jnp.pad(from_above, ((0, stripe_rows - HALO), (0, 0)))
        + jnp.pad(from_below, ((stripe_rows - HALO, 0), (0, 0)))
    )
    gradient = lax.psum_scatter(
        folded.astype(jnp.bfloat16), "exp", scatter_dimension=1, tiled=True
    ).astype(jnp.float32)
    return (gradient, residuals)


def solution(mesh):
    in_specs = (
        P("sky", None),
        P(("sky", "exp"), None, None),
        P(("sky", "exp"), None, None),
        P(("sky", "exp"), None),
        P(("sky", "exp")),
        P(("sky", "exp")),
        P("exp", None),
    )
    out_specs = (P("sky", "exp"), P(("sky", "exp"), None, None))
    return jax.shard_map(shards, mesh=mesh, in_specs=in_specs, out_specs=out_specs, check_vma=False)
```

profile of v0, /device:TPU:0, one launch (start us, length us, event | category | flops | bytes accessed | tf_op | source)
XLA Modules:
  0.0 443.7 jit_solution(5079500784704721920)
XLA Ops:
  10.9 8.1 %all-to-all-start = ((s32[16,1,2]{2,1,0:T(1,128)}), s32[16,1,2]{2,1,0:T(1,128)S(1)}, u32[]{:S(2)}, u32[]{:S(2)}) async-start(s32[16,1,2]{2,1,0:T(1,128)} %bitcast.3), calls=%async_computation | async-start | bytes 16384 | tf_op jit(solution)/shard_map/all_to_all | solution.py:123
  20.9 62.6 %all-gather.2.cloned.1.call-done = bf16[4096,1024]{1,0:T(8,128)(2,1)} async-done(((bf16[256,1024]{1,0:T(8,128)(2,1)}), bf16[4096,1024]{1,0:T(8,128)(2,1)}) %all-gather.2.cloned.1.call-update) | async-done | bytes 8388624 | tf_op jit(solution)/shard_map/all_gather | solution.py:106
  83.5 14.8 %pad.49 = bf16[4136,1064]{1,0:T(8,128)(2,1)} pad(bf16[4096,1024]{1,0:T(8,128)(2,1)} %all-gather.2.cloned.1.call-done, bf16[]{:T(256)} %constant.73.clone.1), padding=20_20x20_20 | pad | bytes 17190018 | tf_op jit(solution)/shard_map/jit(_pad)/pad | solution.py:107
  98.3 58.3 %while.16 = (s32[]{:T(128)}, bf16[4136,1064]{1,0:T(8,128)(2,1)}, s32[16,2]{0,1:T(2,128)S(1)}, bf16[16,168,168]{2,1,0:T(8,128)(2,1)}, s32[]{:T(128)}) while((s32[]{:T(128)}, bf16[4136,1064]{1,0:T(8,128)(2,1)}, s32[16,2]{0,1:T(2,128)S(1)}, bf16[16,168,168]{2,1,0:T(8,128)(2,1)}, s32[]{:T(128)}) %tuple.53), condition=%wide.while_cond, body=%wide.while_body.sunk | while | flops 2 | bytes 173665 | solution.py:112
  99.0 3.0 bitcast_dynamic-update-slice_fusion.4
  102.6 3.0 bitcast_dynamic-update-slice_fusion.4
  106.3 3.0 bitcast_dynamic-update-slice_fusion.4
  109.9 3.0 bitcast_dynamic-update-slice_fusion.4
  113.5 3.0 bitcast_dynamic-update-slice_fusion.4
  117.2 3.0 bitcast_dynamic-update-slice_fusion.4
  120.8 3.0 bitcast_dynamic-update-slice_fusion.4
  124.5 3.0 bitcast_dynamic-update-slice_fusion.4
  128.1 3.0 bitcast_dynamic-update-slice_fusion.4
  131.8 3.0 bitcast_dynamic-update-slice_fusion.4
  135.4 3.0 bitcast_dynamic-update-slice_fusion.4
  139.1 3.0 bitcast_dynamic-update-slice_fusion.4
  142.7 3.0 bitcast_dynamic-update-slice_fusion.4
  146.4 3.0 bitcast_dynamic-update-slice_fusion.4
  150.0 3.0 bitcast_dynamic-update-slice_fusion.4
  153.7 3.0 bitcast_dynamic-update-slice_fusion.4
  156.6 157.8 %while.17 = (s32[]{:T(128)}, bf16[16,128,128]{2,1,0:T(8,128)(2,1)}, f32[16,168,168]{2,1,0:T(8,128)S(1)}, s32[16,128,128]{2,1,0:T(8,128)}, bf16[16,168,168]{2,1,0...) while((s32[]{:T(128)}, bf16[16,128,128]{2,1,0:T(8,128)(2,1)}, ...), condition=%wide.region_3.4_spmd.clone, body=%wide.region_2.3_spmd.clone.sunk | while | flops 1093145856 | bytes 34470920 | solution.py:116
  174.4 1.9 fusion.82
  314.4 2.8 broadcast_in_dim.36
  317.2 4.1 scatter_fusion
  321.4 2.8 convert_element_type.99
  324.2 3.7 copy.17
  327.9 5.2 %all-to-all-start.1 = ((bf16[16,2,168,168]{3,1,2,0:T(2,128)(2,1)}), bf16[16,2,168,168]{3,1,2,0:T(2,128)(2,1)S(1)}, u32[]{:S(2)}, u32[]{:S(2)}) async-start(bf16[16,2,168,168]{3,1,2,0:T(2,128)(2,1)} %copy.17), calls=%async_computation.1 | async-start | bytes 5505024 | tf_op jit(solution)/shard_map/all_to_all | solution.py:120
  334.7 40.4 %all-to-all-done.1 = bf16[16,2,168,168]{3,1,2,0:T(2,128)(2,1)S(1)} async-done(((bf16[16,2,168,168]{3,1,2,0:T(2,128)(2,1)}), bf16[16,2,168,168]{3,1,2,0:T(2,128)(2,1)S(1)}, u32[]{:S(2)}, u32[]{:S(2)}) %all-to-all-start.1) | async-done | bytes 1806368 | tf_op jit(solution)/shard_map/all_to_all | solution.py:120
  375.1 4.7 %copy.18 = bf16[16,2,168,168]{3,1,0,2:T(2,128)(2,1)} copy(bf16[16,2,168,168]{3,1,2,0:T(2,128)(2,1)S(1)} %all-to-all-done.1) | data formatting | bytes 3612672 | tf_op jit(solution)/shard_map/all_to_all | solution.py:120
  379.8 5.7 %reshape.115 = bf16[32,168,168,1]{2,0,1,3:T(8,128)(2,1)S(1)} reshape(bf16[16,2,168,168]{3,1,0,2:T(2,128)(2,1)} %copy.18) | data formatting | bytes 3612672 | tf_op jit(solution)/shard_map/reshape | solution.py:125
  395.3 4.3 collective-permute-done.1
  400.9 34.3 %reduce-scatter.4.cloned.1.call-done = bf16[128,256]{1,0:T(8,128)(2,1)} async-done(((bf16[1024,256]{1,0:T(8,128)(2,1)}), bf16[128,256]{1,0:T(8,128)(2,1)}) %reduce-scatter.4.cloned.1.call-update) | async-done | bytes 65552
  (218 shorter events, 185.5 us)
Async XLA Ops:
  7.2 11.9 %copy-start = (bf16[16,1681]{1,0:T(8,128)(2,1)S(1)}, bf16[16,1681]{1,0:T(8,128)(2,1)}, u32[]{:S(2)}) copy-start(bf16[16,1681]{1,0:T(8,128)(2,1)} %param.15) | copy-start | bytes 161380
  7.2 76.3 %all-gather.2.cloned.1.call-start = ((), (), s32[]{:S(2)}) async-start(), calls=%async_computation.3 | async-start | bytes 8912896 | tf_op jit(solution)/shard_map/all_gather | solution.py:106
  10.9 316.9 %all-to-all-start = ((s32[16,1,2]{2,1,0:T(1,128)}), s32[16,1,2]{2,1,0:T(1,128)S(1)}, u32[]{:S(2)}, u32[]{:S(2)}) async-start(s32[16,1,2]{2,1,0:T(1,128)} %bitcast.3), calls=%async_computation | async-start | bytes 16384 | tf_op jit(solution)/shard_map/all_to_all | solution.py:123
  327.9 47.2 %all-to-all-start.1 = ((bf16[16,2,168,168]{3,1,2,0:T(2,128)(2,1)}), bf16[16,2,168,168]{3,1,2,0:T(2,128)(2,1)S(1)}, u32[]{:S(2)}, u32[]{:S(2)}) async-start(bf16[16,2,168,168]{3,1,2,0:T(2,128)(2,1)} %copy.17), calls=%async_computation.1 | async-start | bytes 5505024 | tf_op jit(solution)/shard_map/all_to_all | solution.py:120
  333.1 102.1 %reduce-scatter.4.cloned.1.call-start = ((), (), s32[]{:S(2)}) async-start(), calls=%async_computation.4 | async-start | bytes 589824
  392.0 44.8 %copy-start.1 = (bf16[16,1681]{1,0:T(8,128)(2,1)S(1)}, bf16[16,1681]{1,0:T(8,128)(2,1)}, u32[]{:S(2)}) copy-start(bf16[16,1681]{1,0:T(8,128)(2,1)} %param.15) | copy-start | bytes 161380
  392.3 3.0 collective-permute-start
  393.6 6.0 %collective-permute-start.1 = (bf16[20,1024]{1,0:T(8,128)(2,1)S(1)}, bf16[20,1024]{1,0:T(8,128)(2,1)S(1)}, u32[]{:S(2)}, u32[]{:S(2)}) collective-permute-start(bf16[20,1024]{1,0:T(8,128)(2,1)S(1)} %get-tuple-element.172), channel_id=1, source_target_pairs={{8,0},{16,8},{24,16},{32,24},{40,32},{48,40},{56,48},{64,56},{72,6... | collective-permute-start | bytes 122888 | tf_op jit(solution)/shard_map/ppermute | solution.py:15
Sparse Core Ops, SparseCore 0:
  10.2 73.3 all-gather.1
  401.0 34.1 reduce-scatter.3
where the time goes:
time: 446 us; the launch traced here: 444 us
  waiting for transfers between devices  143 us (32%)
  local copies, waits for them, and re-layouts  125 us (28%)
  matrix products  77.6 us (17%)
  other arithmetic  67.5 us (15%)
  starting transfers between devices  16.3 us (4%)
  between operations  14.3 us (3%)
    all_gather x1, waiting for transfers between devices, shards(): whole = lax.all_gather(sky_model, 'sky', axis=0, tiled=True)  62.6 us
    dynamic_update_slice x32, other arithmetic, shards(): lax.map(per_piece, (patches, kernels, exposure_data, pixel_mask))  59 us
    gather x48, local copies, waits for them, and re-layouts  58.3 us
    dot_general x32, matrix products, correlate(): jnp.dot(field, banded.reshape(width, PSF * out_cols), preferred_element_t...  45.9 us
    all_to_all x1, waiting for transfers between devices, shards(): lax.all_to_all(outgoing.astype(jnp.bfloat16), 'sky', split_axis=0, concat...  40.4 us
    unnamed x3, waiting for transfers between devices  35 us
    dot_general x32, matrix products, correlate(): jnp.einsum('ab,bcj->caj', kernel, table, preferred_element_type=jnp.float32)  30.2 us
    convert_element_type x16, local copies, waits for them, and re-layouts, correlate(): jnp.einsum('ab,bcj->caj', kernel, table, preferred_element_type=jnp.float32)  20.1 us
  transfers between devices with their start and end apart: 6, of which 5 were waited for; matrix products, arithmetic and copies ran while one was open for 56% of the time, Pallas kernels for 0%

commit v1 on v0

--- a/solution.py
+++ b/solution.py
@@ -7,6 +7,27 @@
 PSF = 41
 HALO = 20
 CAP = 2
+
+
+def ring_gather(shard, axis, dim):
+    size, place, extent = (lax.axis_size(axis), lax.axis_index(axis), shard.shape[dim])
+    right = [(i, (i + 1) % size) for i in range(size)]
+    backward = [(i, (i - 1) % size) for i in range(size)]
+    result = jnp.zeros((*shard.shape[:dim], size * extent, *shard.shape[dim + 1 :]), shard.dtype)
+    result = lax.dynamic_update_slice_in_dim(result, shard, place * extent, axis=dim)
+    from_left = from_right = shard
+    halfway = size // 2
+    for turn in range(1, halfway + 1):
+        from_left = lax.ppermute(from_left, axis, right)
+        result = lax.dynamic_update_slice_in_dim(
+            result, from_left, (place - turn) % size * extent, axis=dim
+        )
+        if turn < size - halfway:
+            from_right = lax.ppermute(from_right, axis, backward)
+            result = lax.dynamic_update_slice_in_dim(
+                result, from_right, (place + turn) % size * extent, axis=dim
+            )
+    return result
 
 
 def from_behind(x, axis, by):
@@ -103,7 +124,7 @@
         adjoint = correlate(widened, kernel[::-1, ::-1], adjoint_table, extent)
         return (residual, adjoint)
 
-    whole = lax.all_gather(sky_model, "sky", axis=0, tiled=True)
+    whole = ring_gather(sky_model, "sky", 0)
     padded = jnp.pad(whole, HALO)
     row_start = (owner_sky * block_rows + block_local // per_row) * B
     col_start = block_local % per_row * B

time: 446 us -> 477 us (1.070)
  starting transfers between devices: 16.3 us -> 50.2 us
  waiting for transfers between devices: 143 us -> 113 us
  local copies, waits for them, and re-layouts: 125 us -> 150 us
    all_gather x1 -> x0, waiting for transfers between devices: 62.6 us -> none  [shards(): whole = lax.all_gather(sky_model, 'sky', axis=0, tiled=True)]
    ppermute x0 -> x15, waiting for transfers between devices: none -> 44.1 us  [the longest x8 43.3 us: ring_gather(): from_left = lax.ppermute(from_left, axis, right)]
    ppermute x0 -> x15, starting transfers between devices: none -> 38.9 us  [the longest x7 37.2 us: ring_gather(): from_right = lax.ppermute(from_right, axis, backward)]
    dynamic_update_slice x0 -> x16, local copies, waits for them, and re-layouts: none -> 21.8 us  [the longest x8 11 us: ring_gather(): lax.dynamic_update_slice_in_dim(result, from_left, (place - turn) % size...]
    all_to_all x1, waiting for transfers between devices: 40.4 us -> 30.5 us  [shards(): lax.all_to_all(outgoing.astype(jnp.bfloat16), 'sky', split_axis=0, concat...]
    unnamed x3 -> x2, waiting for transfers between devices: 35 us -> 33.4 us
  transfers between devices with their start and end apart: 6 -> 20, of which waited for: 5 -> 12; matrix products, arithmetic and copies ran while one was open for 56% -> 58% of each run, Pallas kernels for 0% -> 0%
where the time goes in v1:
time: 477 us; the launch traced here: 474 us
  local copies, waits for them, and re-layouts  150 us (31%)
  waiting for transfers between devices  113 us (24%)
  matrix products  78.2 us (16%)
  other arithmetic  67.5 us (14%)
  starting transfers between devices  50.2 us (11%)
  between operations  14.7 us (3%)
    dynamic_update_slice x32, other arithmetic, shards(): lax.map(per_piece, (patches, kernels, exposure_data, pixel_mask))  59 us
    gather x48, local copies, waits for them, and re-layouts  57.5 us
    dot_general x32, matrix products, correlate(): jnp.dot(field, banded.reshape(width, PSF * out_cols), preferred_element_t...  45.9 us
    ppermute x8, waiting for transfers between devices, ring_gather(): from_left = lax.ppermute(from_left, axis, right)  43.3 us
    ppermute x7, starting transfers between devices, ring_gather(): from_right = lax.ppermute(from_right, axis, backward)  37.2 us
    unnamed x2, waiting for transfers between devices  33.4 us
    all_to_all x1, waiting for transfers between devices, shards(): lax.all_to_all(outgoing.astype(jnp.bfloat16), 'sky', split_axis=0, concat...  30.5 us
    dot_general x32, matrix products, correlate(): jnp.einsum('ab,bcj->caj', kernel, table, preferred_element_type=jnp.float32)  30.2 us
  transfers between devices with their start and end apart: 20, of which 12 were waited for; matrix products, arithmetic and copies ran while one was open for 58% of the time, Pallas kernels for 0%

profile of v1, /device:TPU:0, one launch (start us, length us, event | category | flops | bytes accessed | tf_op | source)
XLA Modules:
  0.0 474.1 jit_solution(7067727903471241547)
XLA Ops:
  8.9 5.0 %collective-permute-start.1 = (bf16[256,1024]{1,0:T(8,128)(2,1)}, bf16[256,1024]{1,0:T(8,128)(2,1)S(1)}, u32[]{:S(2)}, u32[]{:S(2)}) collective-permute-start(bf16[256,1024]{1,0:T(8,128)(2,1)} %param.9), channel_id=1, source_target_pairs={{0,120},{8,0},{16,8},{24,16},{32,24},{40,32},{48,40},{56,48},{64,5... | collective-permute-start | bytes 1572872 | tf_op jit(solution)/shard_map/ppermute | solution.py:26
  13.9 12.1 %collective-permute-done = bf16[256,1024]{1,0:T(8,128)(2,1)S(1)} collective-permute-done((bf16[256,1024]{1,0:T(8,128)(2,1)}, bf16[256,1024]{1,0:T(8,128)(2,1)S(1)}, u32[]{:S(2)}, u32[]{:S(2)}) %collective-permute-start) | collective-permute-done | bytes 524320 | tf_op jit(solution)/shard_map/ppermute | solution.py:21
  26.0 5.3 %collective-permute-start.3 = (bf16[256,1024]{1,0:T(8,128)(2,1)S(1)}, bf16[256,1024]{1,0:T(8,128)(2,1)S(1)}, u32[]{:S(2)}, u32[]{:S(2)}) collective-permute-start(bf16[256,1024]{1,0:T(8,128)(2,1)S(1)} %collective-permute-done.1), channel_id=1, source_target_pairs={{0,120},{8,0},{16,8},{24,16},{32,24},{40,32},{48,40},{56,48},{64,5... | collective-permute-start | bytes 1572872 | tf_op jit(solution)/shard_map/ppermute | solution.py:26
  31.3 11.1 %collective-permute-done.2 = bf16[256,1024]{1,0:T(8,128)(2,1)S(1)} collective-permute-done((bf16[256,1024]{1,0:T(8,128)(2,1)S(1)}, bf16[256,1024]{1,0:T(8,128)(2,1)S(1)}, u32[]{:S(2)}, u32[]{:S(2)}) %collective-permute-start.2) | collective-permute-done | bytes 524320 | tf_op jit(solution)/shard_map/ppermute | solution.py:21
  42.4 5.3 %collective-permute-start.5 = (bf16[256,1024]{1,0:T(8,128)(2,1)S(1)}, bf16[256,1024]{1,0:T(8,128)(2,1)S(1)}, u32[]{:S(2)}, u32[]{:S(2)}) collective-permute-start(bf16[256,1024]{1,0:T(8,128)(2,1)S(1)} %collective-permute-done.3), channel_id=1, source_target_pairs={{0,120},{8,0},{16,8},{24,16},{32,24},{40,32},{48,40},{56,48},{64,5... | collective-permute-start | bytes 1572872 | tf_op jit(solution)/shard_map/ppermute | solution.py:26
  47.7 10.2 %collective-permute-done.4 = bf16[256,1024]{1,0:T(8,128)(2,1)S(1)} collective-permute-done((bf16[256,1024]{1,0:T(8,128)(2,1)S(1)}, bf16[256,1024]{1,0:T(8,128)(2,1)S(1)}, u32[]{:S(2)}, u32[]{:S(2)}) %collective-permute-start.4) | collective-permute-done | bytes 524320 | tf_op jit(solution)/shard_map/ppermute | solution.py:21
  58.8 5.4 %collective-permute-start.7 = (bf16[256,1024]{1,0:T(8,128)(2,1)S(1)}, bf16[256,1024]{1,0:T(8,128)(2,1)}, u32[]{:S(2)}, u32[]{:S(2)}) collective-permute-start(bf16[256,1024]{1,0:T(8,128)(2,1)S(1)} %collective-permute-done.5), channel_id=1, source_target_pairs={{0,120},{8,0},{16,8},{24,16},{32,24},{40,32},{48,40},{56,48},{64,5... | collective-permute-start | bytes 1572872 | tf_op jit(solution)/shard_map/ppermute | solution.py:26
  66.3 3.4 all-to-all-start
  74.7 5.4 %collective-permute-start.9 = (bf16[256,1024]{1,0:T(8,128)(2,1)}, bf16[256,1024]{1,0:T(8,128)(2,1)}, u32[]{:S(2)}, u32[]{:S(2)}) collective-permute-start(bf16[256,1024]{1,0:T(8,128)(2,1)} %collective-permute-done.7), channel_id=1, source_target_pairs={{0,120},{8,0},{16,8},{24,16},{32,24},{40,32},{48,40},{56,48},{64,5... | collective-permute-start | bytes 1572872 | tf_op jit(solution)/shard_map/ppermute | solution.py:26
  80.1 4.4 broadcast_in_dim.42
  92.7 5.0 %collective-permute-start.11 = (bf16[256,1024]{1,0:T(8,128)(2,1)}, bf16[256,1024]{1,0:T(8,128)(2,1)S(1)}, u32[]{:S(2)}, u32[]{:S(2)}) collective-permute-start(bf16[256,1024]{1,0:T(8,128)(2,1)} %collective-permute-done.9), channel_id=1, source_target_pairs={{0,120},{8,0},{16,8},{24,16},{32,24},{40,32},{48,40},{56,48},{64,5... | collective-permute-start | bytes 1572872 | tf_op jit(solution)/shard_map/ppermute | solution.py:26
  104.7 5.7 %collective-permute-start.13 = (bf16[256,1024]{1,0:T(8,128)(2,1)S(1)}, bf16[256,1024]{1,0:T(8,128)(2,1)S(1)}, u32[]{:S(2)}, u32[]{:S(2)}) collective-permute-start(bf16[256,1024]{1,0:T(8,128)(2,1)S(1)} %collective-permute-done.11), channel_id=1, source_target_pairs={{0,120},{8,0},{16,8},{24,16},{32,24},{40,32},{48,40},{56,48},{64,5... | collective-permute-start | bytes 1572872 | tf_op jit(solution)/shard_map/ppermute | solution.py:26
  118.8 6.2 %collective-permute-done.14 = bf16[256,1024]{1,0:T(8,128)(2,1)S(1)} collective-permute-done((bf16[256,1024]{1,0:T(8,128)(2,1)S(1)}, bf16[256,1024]{1,0:T(8,128)(2,1)S(1)}, u32[]{:S(2)}, u32[]{:S(2)}) %collective-permute-start.14) | collective-permute-done | bytes 524320 | tf_op jit(solution)/shard_map/ppermute | solution.py:21
  125.8 14.8 %pad.49 = bf16[4136,1064]{1,0:T(8,128)(2,1)} pad(bf16[4096,1024]{1,0:T(8,128)(2,1)} %constant_dynamic-update-slice_fusion, bf16[]{:T(256)} %constant.161.clone.1), padding=20_20x20_20 | pad | bytes 17190018 | tf_op jit(solution)/shard_map/jit(_pad)/pad | solution.py:128
  140.5 57.5 %while.16 = (s32[]{:T(128)}, bf16[4136,1064]{1,0:T(8,128)(2,1)}, s32[16,2]{0,1:T(2,128)S(1)}, bf16[16,168,168]{2,1,0:T(8,128)(2,1)}, s32[]{:T(128)}) while((s32[]{:T(128)}, bf16[4136,1064]{1,0:T(8,128)(2,1)}, s32[16,2]{0,1:T(2,128)S(1)}, bf16[16,168,168]{2,1,0:T(8,128)(2,1)}, s32[]{:T(128)}) %tuple.53), condition=%wide.while_cond, body=%wide.while_body.sunk | while | flops 2 | bytes 173665 | solution.py:133
  141.2 2.9 bitcast_dynamic-update-slice_fusion.4
  152.0 2.9 bitcast_dynamic-update-slice_fusion.4
  155.6 2.9 bitcast_dynamic-update-slice_fusion.4
  173.5 2.9 bitcast_dynamic-update-slice_fusion.4
  177.1 3.0 bitcast_dynamic-update-slice_fusion.4
  184.3 2.9 bitcast_dynamic-update-slice_fusion.4
  187.9 3.0 bitcast_dynamic-update-slice_fusion.4
  195.1 2.9 bitcast_dynamic-update-slice_fusion.4
  198.0 157.8 %while.17 = (s32[]{:T(128)}, bf16[16,128,128]{2,1,0:T(8,128)(2,1)}, f32[16,168,168]{2,1,0:T(8,128)S(1)}, s32[16,128,128]{2,1,0:T(8,128)}, bf16[16,168,168]{2,1,0...) while((s32[]{:T(128)}, bf16[16,128,128]{2,1,0:T(8,128)(2,1)}, ...), condition=%wide.region_3.4_spmd.clone, body=%wide.region_2.3_spmd.clone.sunk | while | flops 1093145856 | bytes 34470920 | solution.py:137
  358.6 4.2 scatter_fusion
  365.6 3.7 copy.17
  369.3 3.7 all-to-all-start.1
  374.6 30.5 %all-to-all-done.1 = bf16[16,2,168,168]{3,1,2,0:T(2,128)(2,1)S(1)} async-done(((bf16[16,2,168,168]{3,1,2,0:T(2,128)(2,1)}), bf16[16,2,168,168]{3,1,2,0:T(2,128)(2,1)S(1)}, u32[]{:S(2)}, u32[]{:S(2)}) %all-to-all-start.1) | async-done | bytes 1806368 | tf_op jit(solution)/shard_map/all_to_all | solution.py:141
  405.1 4.7 copy.18
  409.8 5.7 %reshape.115 = bf16[32,168,168,1]{2,0,1,3:T(8,128)(2,1)S(1)} reshape(bf16[16,2,168,168]{3,1,0,2:T(2,128)(2,1)} %copy.18) | data formatting | bytes 3612672 | tf_op jit(solution)/shard_map/reshape | solution.py:146
  426.6 4.3 collective-permute-done.16
  432.2 33.4 %reduce-scatter.4.cloned.1.call-done = bf16[128,256]{1,0:T(8,128)(2,1)} async-done(((bf16[1024,256]{1,0:T(8,128)(2,1)}), bf16[128,256]{1,0:T(8,128)(2,1)}) %reduce-scatter.4.cloned.1.call-update) | async-done | bytes 65552
  (282 shorter events, 245.7 us)
Async XLA Ops:
  7.2 66.1 %copy-start = (bf16[16,1681]{1,0:T(8,128)(2,1)S(1)}, bf16[16,1681]{1,0:T(8,128)(2,1)}, u32[]{:S(2)}) copy-start(bf16[16,1681]{1,0:T(8,128)(2,1)} %param.15) | copy-start | bytes 161380
  7.2 18.8 %collective-permute-start = (bf16[256,1024]{1,0:T(8,128)(2,1)}, bf16[256,1024]{1,0:T(8,128)(2,1)S(1)}, u32[]{:S(2)}, u32[]{:S(2)}) collective-permute-start(bf16[256,1024]{1,0:T(8,128)(2,1)} %param.9), channel_id=1, source_target_pairs={{0,8},{8,16},{16,24},{24,32},{32,40},{40,48},{48,56},{56,64},{64,7... | collective-permute-start | bytes 1572872 | tf_op jit(solution)/shard_map/ppermute | solution.py:21
  8.9 17.1 %collective-permute-start.1 = (bf16[256,1024]{1,0:T(8,128)(2,1)}, bf16[256,1024]{1,0:T(8,128)(2,1)S(1)}, u32[]{:S(2)}, u32[]{:S(2)}) collective-permute-start(bf16[256,1024]{1,0:T(8,128)(2,1)} %param.9), channel_id=1, source_target_pairs={{0,120},{8,0},{16,8},{24,16},{32,24},{40,32},{48,40},{56,48},{64,5... | collective-permute-start | bytes 1572872 | tf_op jit(solution)/shard_map/ppermute | solution.py:26
  26.0 31.9 %copy-start.6 = (bf16[256,1024]{1,0:T(8,128)(2,1)}, bf16[256,1024]{1,0:T(8,128)(2,1)S(1)}, u32[]{:S(2)}) copy-start(bf16[256,1024]{1,0:T(8,128)(2,1)S(1)} %collective-permute-done) | copy-start | bytes 1572868
  26.0 16.4 %collective-permute-start.2 = (bf16[256,1024]{1,0:T(8,128)(2,1)S(1)}, bf16[256,1024]{1,0:T(8,128)(2,1)S(1)}, u32[]{:S(2)}, u32[]{:S(2)}) collective-permute-start(bf16[256,1024]{1,0:T(8,128)(2,1)S(1)} %collective-permute-done), channel_id=1, source_target_pairs={{0,8},{8,16},{16,24},{24,32},{32,40},{40,48},{48,56},{56,64},{64,7... | collective-permute-start | bytes 1572872 | tf_op jit(solution)/shard_map/ppermute | solution.py:21
  26.0 58.5 %copy-start.7 = (bf16[256,1024]{1,0:T(8,128)(2,1)}, bf16[256,1024]{1,0:T(8,128)(2,1)S(1)}, u32[]{:S(2)}) copy-start(bf16[256,1024]{1,0:T(8,128)(2,1)S(1)} %collective-permute-done.1) | copy-start | bytes 1572868
  26.0 16.4 %collective-permute-start.3 = (bf16[256,1024]{1,0:T(8,128)(2,1)S(1)}, bf16[256,1024]{1,0:T(8,128)(2,1)S(1)}, u32[]{:S(2)}, u32[]{:S(2)}) collective-permute-start(bf16[256,1024]{1,0:T(8,128)(2,1)S(1)} %collective-permute-done.1), channel_id=1, source_target_pairs={{0,120},{8,0},{16,8},{24,16},{32,24},{40,32},{48,40},{56,48},{64,5... | collective-permute-start | bytes 1572872 | tf_op jit(solution)/shard_map/ppermute | solution.py:26
  42.4 5.4 %copy-start.10 = (bf16[256,1024]{1,0:T(8,128)(2,1)}, bf16[256,1024]{1,0:T(8,128)(2,1)S(1)}, u32[]{:S(2)}) copy-start(bf16[256,1024]{1,0:T(8,128)(2,1)S(1)} %collective-permute-done.2) | copy-start | bytes 1572868
  42.4 15.5 %collective-permute-start.4 = (bf16[256,1024]{1,0:T(8,128)(2,1)S(1)}, bf16[256,1024]{1,0:T(8,128)(2,1)S(1)}, u32[]{:S(2)}, u32[]{:S(2)}) collective-permute-start(bf16[256,1024]{1,0:T(8,128)(2,1)S(1)} %collective-permute-done.2), channel_id=1, source_target_pairs={{0,8},{8,16},{16,24},{24,32},{32,40},{40,48},{48,56},{56,64},{64,7... | collective-permute-start | bytes 1572872 | tf_op jit(solution)/shard_map/ppermute | solution.py:21
  42.4 42.1 %copy-start.5 = (bf16[256,1024]{1,0:T(8,128)(2,1)}, bf16[256,1024]{1,0:T(8,128)(2,1)S(1)}, u32[]{:S(2)}) copy-start(bf16[256,1024]{1,0:T(8,128)(2,1)S(1)} %collective-permute-done.3) | copy-start | bytes 1572868
  42.4 16.4 %collective-permute-start.5 = (bf16[256,1024]{1,0:T(8,128)(2,1)S(1)}, bf16[256,1024]{1,0:T(8,128)(2,1)S(1)}, u32[]{:S(2)}, u32[]{:S(2)}) collective-permute-start(bf16[256,1024]{1,0:T(8,128)(2,1)S(1)} %collective-permute-done.3), channel_id=1, source_target_pairs={{0,120},{8,0},{16,8},{24,16},{32,24},{40,32},{48,40},{56,48},{64,5... | collective-permute-start | bytes 1572872 | tf_op jit(solution)/shard_map/ppermute | solution.py:26
  57.9 14.6 %collective-permute-start.6 = (bf16[256,1024]{1,0:T(8,128)(2,1)S(1)}, bf16[256,1024]{1,0:T(8,128)(2,1)S(1)}, u32[]{:S(2)}, u32[]{:S(2)}) collective-permute-start(bf16[256,1024]{1,0:T(8,128)(2,1)S(1)} %collective-permute-done.4), channel_id=1, source_target_pairs={{0,8},{8,16},{16,24},{24,32},{32,40},{40,48},{48,56},{56,64},{64,7... | collective-permute-start | bytes 1572872 | tf_op jit(solution)/shard_map/ppermute | solution.py:21
  58.8 25.7 %copy-start.3 = (bf16[256,1024]{1,0:T(8,128)(2,1)}, bf16[256,1024]{1,0:T(8,128)(2,1)S(1)}, u32[]{:S(2)}) copy-start(bf16[256,1024]{1,0:T(8,128)(2,1)S(1)} %collective-permute-done.5) | copy-start | bytes 1572868
  58.8 15.9 %collective-permute-start.7 = (bf16[256,1024]{1,0:T(8,128)(2,1)S(1)}, bf16[256,1024]{1,0:T(8,128)(2,1)}, u32[]{:S(2)}, u32[]{:S(2)}) collective-permute-start(bf16[256,1024]{1,0:T(8,128)(2,1)S(1)} %collective-permute-done.5), channel_id=1, source_target_pairs={{0,120},{8,0},{16,8},{24,16},{32,24},{40,32},{48,40},{56,48},{64,5... | collective-permute-start | bytes 1572872 | tf_op jit(solution)/shard_map/ppermute | solution.py:26
  66.3 302.9 %all-to-all-start = ((s32[16,1,2]{2,1,0:T(1,128)}), s32[16,1,2]{2,1,0:T(1,128)S(1)}, u32[]{:S(2)}, u32[]{:S(2)}) async-start(s32[16,1,2]{2,1,0:T(1,128)} %bitcast.3), calls=%async_computation | async-start | bytes 16384 | tf_op jit(solution)/shard_map/all_to_all | solution.py:144
  72.5 12.0 %copy-start.8 = (bf16[256,1024]{1,0:T(8,128)(2,1)}, bf16[256,1024]{1,0:T(8,128)(2,1)S(1)}, u32[]{:S(2)}) copy-start(bf16[256,1024]{1,0:T(8,128)(2,1)S(1)} %collective-permute-done.6) | copy-start | bytes 1572868
  72.5 13.8 %collective-permute-start.8 = (bf16[256,1024]{1,0:T(8,128)(2,1)S(1)}, bf16[256,1024]{1,0:T(8,128)(2,1)}, u32[]{:S(2)}, u32[]{:S(2)}) collective-permute-start(bf16[256,1024]{1,0:T(8,128)(2,1)S(1)} %collective-permute-done.6), channel_id=1, source_target_pairs={{0,8},{8,16},{16,24},{24,32},{32,40},{40,48},{48,56},{56,64},{64,7... | collective-permute-start | bytes 1572872 | tf_op jit(solution)/shard_map/ppermute | solution.py:21
  74.7 9.8 %copy-start.2 = (bf16[256,1024]{1,0:T(8,128)(2,1)S(1)}, bf16[256,1024]{1,0:T(8,128)(2,1)}, u32[]{:S(2)}) copy-start(bf16[256,1024]{1,0:T(8,128)(2,1)} %param.9) | copy-start | bytes 1572868
  74.7 11.9 %copy-start.11 = (bf16[16,1681]{1,0:T(8,128)(2,1)S(1)}, bf16[16,1681]{1,0:T(8,128)(2,1)}, u32[]{:S(2)}) copy-start(bf16[16,1681]{1,0:T(8,128)(2,1)} %convolution_convert_fusion) | copy-start | bytes 161380
  74.7 17.9 %collective-permute-start.9 = (bf16[256,1024]{1,0:T(8,128)(2,1)}, bf16[256,1024]{1,0:T(8,128)(2,1)}, u32[]{:S(2)}, u32[]{:S(2)}) collective-permute-start(bf16[256,1024]{1,0:T(8,128)(2,1)} %collective-permute-done.7), channel_id=1, source_target_pairs={{0,120},{8,0},{16,8},{24,16},{32,24},{40,32},{48,40},{56,48},{64,5... | collective-permute-start | bytes 1572872 | tf_op jit(solution)/shard_map/ppermute | solution.py:26
  86.3 13.3 %collective-permute-start.10 = (bf16[256,1024]{1,0:T(8,128)(2,1)}, bf16[256,1024]{1,0:T(8,128)(2,1)}, u32[]{:S(2)}, u32[]{:S(2)}) collective-permute-start(bf16[256,1024]{1,0:T(8,128)(2,1)} %collective-permute-done.8), channel_id=1, source_target_pairs={{0,8},{8,16},{16,24},{24,32},{32,40},{40,48},{48,56},{56,64},{64,7... | collective-permute-start | bytes 1572872 | tf_op jit(solution)/shard_map/ppermute | solution.py:21
  86.9 13.5 %copy-start.4 = (bf16[256,1024]{1,0:T(8,128)(2,1)S(1)}, bf16[256,1024]{1,0:T(8,128)(2,1)}, u32[]{:S(2)}) copy-start(bf16[256,1024]{1,0:T(8,128)(2,1)} %copy-done.3) | copy-start | bytes 1572868
  86.9 14.3 %copy-start.9 = (bf16[256,1024]{1,0:T(8,128)(2,1)S(1)}, bf16[256,1024]{1,0:T(8,128)(2,1)}, u32[]{:S(2)}) copy-start(bf16[256,1024]{1,0:T(8,128)(2,1)} %copy-done.8) | copy-start | bytes 1572868
  92.7 12.1 %collective-permute-start.11 = (bf16[256,1024]{1,0:T(8,128)(2,1)}, bf16[256,1024]{1,0:T(8,128)(2,1)S(1)}, u32[]{:S(2)}, u32[]{:S(2)}) collective-permute-start(bf16[256,1024]{1,0:T(8,128)(2,1)} %collective-permute-done.9), channel_id=1, source_target_pairs={{0,120},{8,0},{16,8},{24,16},{32,24},{40,32},{48,40},{56,48},{64,5... | collective-permute-start | bytes 1572872 | tf_op jit(solution)/shard_map/ppermute | solution.py:26
  99.6 12.8 %collective-permute-start.12 = (bf16[256,1024]{1,0:T(8,128)(2,1)}, bf16[256,1024]{1,0:T(8,128)(2,1)S(1)}, u32[]{:S(2)}, u32[]{:S(2)}) collective-permute-start(bf16[256,1024]{1,0:T(8,128)(2,1)} %collective-permute-done.10), channel_id=1, source_target_pairs={{0,8},{8,16},{16,24},{24,32},{32,40},{40,48},{48,56},{56,64},{64,7... | collective-permute-start | bytes 1572872 | tf_op jit(solution)/shard_map/ppermute | solution.py:21
  104.7 13.2 %collective-permute-start.13 = (bf16[256,1024]{1,0:T(8,128)(2,1)S(1)}, bf16[256,1024]{1,0:T(8,128)(2,1)S(1)}, u32[]{:S(2)}, u32[]{:S(2)}) collective-permute-start(bf16[256,1024]{1,0:T(8,128)(2,1)S(1)} %collective-permute-done.11), channel_id=1, source_target_pairs={{0,120},{8,0},{16,8},{24,16},{32,24},{40,32},{48,40},{56,48},{64,5... | collective-permute-start | bytes 1572872 | tf_op jit(solution)/shard_map/ppermute | solution.py:26
  112.4 12.5 %collective-permute-start.14 = (bf16[256,1024]{1,0:T(8,128)(2,1)S(1)}, bf16[256,1024]{1,0:T(8,128)(2,1)S(1)}, u32[]{:S(2)}, u32[]{:S(2)}) collective-permute-start(bf16[256,1024]{1,0:T(8,128)(2,1)S(1)} %collective-permute-done.12), channel_id=1, source_target_pairs={{0,8},{8,16},{16,24},{24,32},{32,40},{40,48},{48,56},{56,64},{64,7... | collective-permute-start | bytes 1572872 | tf_op jit(solution)/shard_map/ppermute | solution.py:21
  369.3 35.9 %all-to-all-start.1 = ((bf16[16,2,168,168]{3,1,2,0:T(2,128)(2,1)}), bf16[16,2,168,168]{3,1,2,0:T(2,128)(2,1)S(1)}, u32[]{:S(2)}, u32[]{:S(2)}) async-start(bf16[16,2,168,168]{3,1,2,0:T(2,128)(2,1)} %copy.17), calls=%async_computation.1 | async-start | bytes 5505024 | tf_op jit(solution)/shard_map/all_to_all | solution.py:141
  373.0 92.6 %reduce-scatter.4.cloned.1.call-start = ((), (), s32[]{:S(2)}) async-start(), calls=%async_computation.3 | async-start | bytes 589824
  422.0 45.2 %copy-start.1 = (bf16[16,1681]{1,0:T(8,128)(2,1)S(1)}, bf16[16,1681]{1,0:T(8,128)(2,1)}, u32[]{:S(2)}) copy-start(bf16[16,1681]{1,0:T(8,128)(2,1)} %param.15) | copy-start | bytes 161380
  422.3 4.3 collective-permute-start.15
  424.9 6.0 %collective-permute-start.16 = (bf16[20,1024]{1,0:T(8,128)(2,1)S(1)}, bf16[20,1024]{1,0:T(8,128)(2,1)S(1)}, u32[]{:S(2)}, u32[]{:S(2)}) collective-permute-start(bf16[20,1024]{1,0:T(8,128)(2,1)S(1)} %get-tuple-element.172), channel_id=1, source_target_pairs={{8,0},{16,8},{24,16},{32,24},{40,32},{48,40},{56,48},{64,56},{72,6... | collective-permute-start | bytes 122888 | tf_op jit(solution)/shard_map/ppermute | solution.py:36
Sparse Core Ops, SparseCore 0:
  432.3 33.2 reduce-scatter.3
